TPU v7x, 512 devices: a whole 4x4x16 slice. The times are simulated.
512 devices in a mesh: col: 64 (over y, z), row: 8 (over x, core).
Axes of the slice: x: 4, y: 4, z: 16, core: 2. Of those that a mesh axis runs over, the one named last changes fastest.
Arguments:
- x_block: bfloat16 [8, 8192, 64], P('row', 'col'), may hold values from -6 to 6
- tiles: bfloat16 [64, 8, 96, 128, 128], P('col', 'row'), may hold values from -0.078125 to 0.078125
- tile_rows: int32 [64, 8, 96], P('col', 'row'), may hold values from 0 to 63
- tile_cols: int32 [64, 8, 96], P('col', 'row'), may hold values from 0 to 7
- tile_count: int32 [64, 8], P('col', 'row'), may hold values from 1 to 96, as said below
Outputs:
- filtered: bfloat16 [8, 8192, 64], P('row', 'col')
- gram: float32 [64, 64], replicated
Inputs may be any that keep to these rules, and one draw needn't show every extreme that they name: `tile_count`: padding slots hold arbitrary tiles and indices; every draw has some device with all 96 slots live.
All inputs are finite; a program needn't handle non-finite values.
Results may differ from a plain program's by a relative error of at most 0.0049.
Values may be sent and summed in bfloat16 or wider, within the bound.
A program may use at most 64 MiB of HBM per device.

v0:
```python
import jax
import jax.numpy as jnp
from jax import lax
from jax.sharding import PartitionSpec as P


def local(x_block, tiles, tile_rows, tile_cols, tile_count):
    n_col = lax.axis_size("col")
    n_row = lax.axis_size("row")
    tile_data = tiles[0, 0]
    rows_here = tile_rows[0, 0]
    cols_here = tile_cols[0, 0]
    count_here = tile_count[0, 0]
    vectors = x_block.shape[2]
    slots = tile_data.shape[0]
    live = jnp.arange(slots, dtype=jnp.int32) < count_here
    placing = (
        (rows_here[None, :] == jnp.arange(n_col, dtype=jnp.int32)[:, None]) & live[None, :]
    ).astype(jnp.float32)

    def apply_local(segment):
        slab_vecs = lax.all_gather(segment[0], "row", axis=0, tiled=True)
        picked = slab_vecs.reshape(n_row, 128, vectors)[cols_here]
        products = jnp.einsum("tij,tjk->tik", tile_data, picked, preferred_element_type=jnp.float32)
        products = products.reshape(slots, 128 * vectors)
        band_sums = jnp.dot(placing, products, precision=lax.Precision.HIGH)
        owned = lax.psum_scatter(band_sums, "col", scatter_dimension=0, tiled=True)
        return owned.reshape(1, 128, vectors)

    first = apply_local(x_block).astype(jnp.bfloat16)
    second = apply_local(first)
    gram_term = jnp.dot(first[0].astype(jnp.float32).T, second[0], precision=lax.Precision.HIGHEST)
    gram = lax.psum(gram_term, ("col", "row")) / (n_col * n_row * 128)
    return (second.astype(jnp.bfloat16), gram)


def solution(mesh):
    placed = (
        P("row", "col", None),
        P("col", "row", None, None, None),
        P("col", "row", None),
        P("col", "row", None),
        P("col", "row"),
    )
    return jax.shard_map(
        local, mesh=mesh, in_specs=placed, out_specs=(P("row", "col", None), P()), check_vma=False
    )
```

profile of v0, /device:TPU:1, one launch (start us, length us, event | category | flops | bytes accessed | tf_op | source)
XLA Modules:
  0.0 760.7 jit_solution(15123610081769181831)
XLA Ops:
  7.2 0.0 copy-start
  7.2 0.0 all-reduce.5.cloned.1.call-start
  8.0 0.7 fusion.20
  8.8 18.2 %all-gather = bf16[1,1024,64]{1,2,0:T(8,128)(2,1)S(1)} all-gather(bf16[1,128,64]{1,2,0:T(8,128)(2,1)} %param.5), channel_id=2, replica_groups=mesh['col'=64,'row'=8] {'row'}, dimensions={1}, use_global_device_ids=true | all-gather | bytes 147456 | tf_op jit(solution)/shard_map/all_gather | solution.py:22
  27.1 2.0 gather_fusion
  29.0 0.0 copy-done
  29.0 5.3 fusion.4
  34.4 0.0 copy-start.3
  34.4 5.1 copy.18
  39.4 0.0 copy-done.3
  39.4 5.1 fusion.14
  44.5 250.4 %all-reduce.6 = bf16[64,8192]{1,0:T(8,128)(2,1)} all-reduce(f32[64,8192]{1,0:T(8,128)} %fusion.14), channel_id=3, replica_groups=mesh['col'=64,'row'=8] {'col'}, use_global_device_ids=true, to_apply=%region_0.0.clone | all-reduce | flops 524288 | bytes 3145728
  294.9 1.3 dynamic-slice
  296.2 1.7 fusion.10
  297.9 0.1 convert_element_type.27
  298.0 0.0 copy-start.1
  298.0 66.5 %all_gather.7 = bf16[1024,64]{1,0:T(8,128)(2,1)S(1)} all-gather(bf16[128,64]{1,0:T(8,128)(2,1)S(1)} %convert_element_type.27), channel_id=1, replica_groups=mesh['col'=64,'row'=8] {'row'}, dimensions={0}, use_global_device_ids=true | all-gather | bytes 147456 | tf_op jit(solution)/shard_map/all_gather | solution.py:22
  364.5 0.0 copy-done.1
  364.5 0.1 copy.20
  364.6 2.0 gather_fusion.1
  366.6 5.3 fusion.7
  371.9 5.1 copy.21
  377.0 0.0 copy-start.2
  377.0 5.1 fusion.12
  382.0 0.0 all-reduce.5.cloned.1.call-update
  382.1 257.0 %all-reduce.5.cloned.1.call-done = f32[64,8192]{1,0:T(8,128)} async-done(((f32[64,8192]{1,0:T(8,128)}), f32[64,8192]{1,0:T(8,128)}) %all-reduce.5.cloned.1.call-update) | async-done | bytes 2097168
  639.1 1.7 convert_reduce_fusion
  640.8 0.1 convert_element_type.29
  640.9 0.7 copy.22
  641.6 1.7 dynamic-slice_reduce_fusion
  643.3 0.1 squeeze_reshape.3
  643.4 0.0 copy-done.2
  643.4 0.2 fusion.21
  643.6 109.7 %psum.7 = f32[64,64]{1,0:T(8,128)S(1)} all-reduce(f32[64,64]{1,0:T(8,128)S(1)} %fusion.21), channel_id=1, replica_groups=mesh['col'=64,'row'=8] {'col','row'}, use_global_device_ids=true, to_apply=%region_2.0 | all-reduce | flops 4096 | bytes 32768 | tf_op jit(solution)/shard_map/psum | solution.py:33
  753.3 0.6 broadcast_multiply_fusion
  (4 shorter events, 0.1 us)
Async XLA Ops:
  7.2 21.8 %copy-start = (bf16[1,1,96,128,128]{4,3,2,1,0:T(8,128)(2,1)S(1)}, bf16[1,1,96,128,128]{4,3,2,1,0:T(8,128)(2,1)}, u32[]{:S(2)}) copy-start(bf16[1,1,96,128,128]{4,3,2,1,0:T(8,128)(2,1)} %param.6) | copy-start | bytes 9437188
  7.2 631.9 %all-reduce.5.cloned.1.call-start = ((), (), s32[]{:S(2)}) async-start(), calls=%async_computation | async-start | bytes 4194304
  34.4 5.1 copy-start.3
  298.0 66.5 %copy-start.1 = (bf16[128,64]{1,0:T(8,128)(2,1)}, bf16[128,64]{1,0:T(8,128)(2,1)S(1)}, u32[]{:S(2)}) copy-start(bf16[128,64]{1,0:T(8,128)(2,1)S(1)} %convert_element_type.27) | copy-start | bytes 49156
  377.0 266.4 %copy-start.2 = (bf16[128,64]{1,0:T(8,128)(2,1)S(1)}, bf16[128,64]{1,0:T(8,128)(2,1)}, u32[]{:S(2)}) copy-start(bf16[128,64]{1,0:T(8,128)(2,1)} %copy-done.1) | copy-start | bytes 49156
Sparse Core Ops, SparseCore 0:
  382.2 256.8 all-reduce.4
where the time goes:
time: 761 us
  blocking collectives  445 us (58%)
  waiting for transfers between devices  257 us (34%)
  local copies, waits for them, and re-layouts  21.7 us (3%)
  matrix products  21 us (3%)
  between operations  14.9 us (2%)
    unnamed x2, waiting for transfers between devices  257 us
    unnamed x1, blocking collectives  250 us
    psum x1, blocking collectives, local(): gram = lax.psum(gram_term, ('col', 'row')) / (n_col * n_row * 128)  110 us
    all_gather x2, blocking collectives, apply_local(): slab_vecs = lax.all_gather(segment[0], 'row', axis=0, tiled=True)  84.7 us
  transfers between devices with their start and end apart: 1, of which 1 were waited for; matrix products, arithmetic and copies ran while one was open for 0% of the time, Pallas kernels for 0%

commit v1 on v0

--- a/solution.py
+++ b/solution.py
@@ -30,7 +30,7 @@
     first = apply_local(x_block).astype(jnp.bfloat16)
     second = apply_local(first)
     gram_term = jnp.dot(first[0].astype(jnp.float32).T, second[0], precision=lax.Precision.HIGHEST)
-    gram = lax.psum(gram_term, ("col", "row")) / (n_col * n_row * 128)
+    gram = jnp.sum(jax.lax.all_gather(gram_term, ("col", "row")), axis=0) / (n_col * n_row * 128)
     return (second.astype(jnp.bfloat16), gram)
 
 

time: 761 us -> 885 us (1.16)
  waiting for transfers between devices: 257 us -> 483 us
  blocking collectives: 445 us -> 335 us
    all_gather x0 -> x1, waiting for transfers between devices: none -> 225 us  [local(): jax.lax.all_gather(gram_term, ('col', 'row'))]
    psum x1 -> x0, blocking collectives: 110 us -> none  [local(): gram = lax.psum(gram_term, ('col', 'row')) / (n_col * n_row * 128)]
    unnamed x2 -> x3, waiting for transfers between devices: 257 us -> 258 us
  transfers between devices with their start and end apart: 1 -> 2, of which waited for: 1 -> 2; matrix products, arithmetic and copies ran while one was open for 0% -> 0% of each run, Pallas kernels for 0% -> 0%
where the time goes in v1:
time: 885 us; the launch traced here: 884 us
  waiting for transfers between devices  483 us (55%)
  blocking collectives  335 us (38%)
  matrix products  21.7 us (2%)
  local copies, waits for them, and re-layouts  21.5 us (2%)
  between operations  14.9 us (2%)
    unnamed x3, waiting for transfers between devices  258 us
    unnamed x1, blocking collectives  250 us
    all_gather x1, waiting for transfers between devices, local(): jax.lax.all_gather(gram_term, ('col', 'row'))  225 us
    all_gather x2, blocking collectives, apply_local(): slab_vecs = lax.all_gather(segment[0], 'row', axis=0, tiled=True)  84.7 us
  transfers between devices with their start and end apart: 2, of which 2 were waited for; matrix products, arithmetic and copies ran while one was open for 0% of the time, Pallas kernels for 0%

profile of v1, /device:TPU:1, one launch (start us, length us, event | category | flops | bytes accessed | tf_op | source)
XLA Modules:
  0.0 884.2 jit_solution(2235849170609126572)
XLA Ops:
  7.2 0.0 copy-start
  7.2 0.0 all-reduce.5.cloned.1.call-start
  8.0 0.7 fusion.20
  8.8 18.2 %all-gather = bf16[1,1024,64]{1,2,0:T(8,128)(2,1)S(1)} all-gather(bf16[1,128,64]{1,2,0:T(8,128)(2,1)} %param.5), channel_id=2, replica_groups=mesh['col'=64,'row'=8] {'row'}, dimensions={1}, use_global_device_ids=true | all-gather | bytes 147456 | tf_op jit(solution)/shard_map/all_gather | solution.py:22
  27.1 2.0 gather_fusion
  29.0 0.0 copy-done
  29.0 5.3 fusion.4
  34.4 0.0 copy-start.3
  34.4 5.1 copy.18
  39.4 0.0 copy-done.3
  39.4 5.1 fusion.14
  44.5 250.4 %all-reduce.6 = bf16[64,8192]{1,0:T(8,128)(2,1)} all-reduce(f32[64,8192]{1,0:T(8,128)} %fusion.14), channel_id=4, replica_groups=mesh['col'=64,'row'=8] {'col'}, use_global_device_ids=true, to_apply=%region_0.0.clone | all-reduce | flops 524288 | bytes 3145728
  294.9 1.3 dynamic-slice
  296.1 1.7 fusion.10
  297.8 0.1 convert_element_type.27
  297.9 0.0 copy-start.1
  297.9 66.5 %all_gather.13 = bf16[1024,64]{1,0:T(8,128)(2,1)S(1)} all-gather(bf16[128,64]{1,0:T(8,128)(2,1)S(1)} %convert_element_type.27), channel_id=1, replica_groups=mesh['col'=64,'row'=8] {'row'}, dimensions={0}, use_global_device_ids=true | all-gather | bytes 147456 | tf_op jit(solution)/shard_map/all_gather | solution.py:22
  364.3 0.0 copy-done.1
  364.4 0.1 copy.20
  364.5 2.0 gather_fusion.1
  366.4 5.3 fusion.7
  371.8 5.1 copy.21
  376.8 0.0 copy-start.2
  376.8 5.1 fusion.12
  381.9 0.0 all-reduce.5.cloned.1.call-update
  382.0 0.0 all-gather.4.cloned.1.call-start
  382.0 257.5 %all-reduce.5.cloned.1.call-done = f32[64,8192]{1,0:T(8,128)} async-done(((f32[64,8192]{1,0:T(8,128)}), f32[64,8192]{1,0:T(8,128)}) %all-reduce.5.cloned.1.call-update) | async-done | bytes 2097168
  639.6 1.7 dynamic-slice_reduce_fusion
  641.2 0.1 squeeze_reshape.3
  641.3 0.0 copy-done.2
  641.3 0.8 fusion.21
  642.1 0.0 all-gather.4.cloned.1.call-update
  642.2 1.7 convert_reduce_fusion
  643.9 0.1 convert_element_type.29
  644.0 0.7 copy.22
  644.7 225.1 %all-gather.4.cloned.1.call-done = f32[32768,64]{1,0:T(8,128)} async-done(((f32[64,64]{1,0:T(8,128)}), f32[32768,64]{1,0:T(8,128)}) %all-gather.4.cloned.1.call-update) | async-done | bytes 8388624 | tf_op jit(solution)/shard_map/all_gather | solution.py:33
  869.8 6.9 reduce_sum.9
  876.7 0.6 broadcast_multiply_fusion
  (4 shorter events, 0.1 us)
Async XLA Ops:
  7.2 21.8 %copy-start = (bf16[1,1,96,128,128]{4,3,2,1,0:T(8,128)(2,1)S(1)}, bf16[1,1,96,128,128]{4,3,2,1,0:T(8,128)(2,1)}, u32[]{:S(2)}) copy-start(bf16[1,1,96,128,128]{4,3,2,1,0:T(8,128)(2,1)} %param.6) | copy-start | bytes 9437188
  7.2 632.4 %all-reduce.5.cloned.1.call-start = ((), (), s32[]{:S(2)}) async-start(), calls=%async_computation.1 | async-start | bytes 4194304
  34.4 5.1 copy-start.3
  297.9 66.5 %copy-start.1 = (bf16[128,64]{1,0:T(8,128)(2,1)}, bf16[128,64]{1,0:T(8,128)(2,1)S(1)}, u32[]{:S(2)}) copy-start(bf16[128,64]{1,0:T(8,128)(2,1)S(1)} %convert_element_type.27) | copy-start | bytes 49156
  376.8 264.5 %copy-start.2 = (bf16[128,64]{1,0:T(8,128)(2,1)S(1)}, bf16[128,64]{1,0:T(8,128)(2,1)}, u32[]{:S(2)}) copy-start(bf16[128,64]{1,0:T(8,128)(2,1)} %copy-done.1) | copy-start | bytes 49156
  382.0 487.8 %all-gather.4.cloned.1.call-start = ((), (), s32[]{:S(2)}) async-start(), calls=%async_computation | async-start | bytes 16809984 | tf_op jit(solution)/shard_map/all_gather | solution.py:33
Sparse Core Ops, SparseCore 0:
  382.1 257.4 all-reduce.4
  645.5 224.1 all-gather.3

commit v2 on v0

--- a/solution.py
+++ b/solution.py
@@ -19,7 +19,18 @@
     ).astype(jnp.float32)
 
     def apply_local(segment):
-        slab_vecs = lax.all_gather(segment[0], "row", axis=0, tiled=True)
+        z_new = segment[0]
+        n_lanes = lax.axis_size("row")
+        leaves = [z_new]
+        rr = 0
+        item_now = [(h - 1, h) for h in range(1, n_lanes)] + [(n_lanes - 1, 0)]
+        while rr < n_lanes - 1:
+            z_new = lax.ppermute(z_new, axis_name="row", perm=item_now)
+            leaves += [z_new]
+            rr += 1
+        slab_vecs = jnp.roll(
+            jnp.concatenate([*reversed(leaves)], 0), (lax.axis_index("row") + 1) * z_new.shape[0], 0
+        )
         picked = slab_vecs.reshape(n_row, 128, vectors)[cols_here]
         products = jnp.einsum("tij,tjk->tik", tile_data, picked, preferred_element_type=jnp.float32)
         products = products.reshape(slots, 128 * vectors)

time: 761 us -> 796 us (1.046)
  blocking collectives: 445 us -> 359 us
  waiting for transfers between devices: 257 us -> 320 us
  starting transfers between devices: 0.04 us -> 56.3 us
    all_gather x2 -> x0, blocking collectives: 84.7 us -> none  [apply_local(): slab_vecs = lax.all_gather(segment[0], 'row', axis=0, tiled=True)]
    ppermute x0 -> x14, waiting for transfers between devices: none -> 60.7 us  [apply_local(): z_new = lax.ppermute(z_new, axis_name='row', perm=item_now)]
    ppermute x0 -> x14, starting transfers between devices: none -> 56.2 us  [apply_local(): z_new = lax.ppermute(z_new, axis_name='row', perm=item_now)]
  transfers between devices with their start and end apart: 1 -> 15, of which waited for: 1 -> 15; matrix products, arithmetic and copies ran while one was open for 0% -> 0% of each run, Pallas kernels for 0% -> 0%
where the time goes in v2:
time: 796 us
  blocking collectives  359 us (45%)
  waiting for transfers between devices  320 us (40%)
  starting transfers between devices  56.3 us (7%)
  local copies, waits for them, and re-layouts  22.4 us (3%)
  matrix products  21 us (3%)
  between operations  14.8 us (2%)
    unnamed x2, waiting for transfers between devices  260 us
    unnamed x1, blocking collectives  249 us
    psum x1, blocking collectives, local(): gram = lax.psum(gram_term, ('col', 'row')) / (n_col * n_row * 128)  110 us
    ppermute x14, waiting for transfers between devices, apply_local(): z_new = lax.ppermute(z_new, axis_name='row', perm=item_now)  60.7 us
    ppermute x14, starting transfers between devices, apply_local(): z_new = lax.ppermute(z_new, axis_name='row', perm=item_now)  56.2 us
  transfers between devices with their start and end apart: 15, of which 15 were waited for; matrix products, arithmetic and copies ran while one was open for 0% of the time, Pallas kernels for 0%

profile of v2, /device:TPU:1, one launch (start us, length us, event | category | flops | bytes accessed | tf_op | source)
XLA Modules:
  0.0 795.8 jit_solution(346837555472726104)
XLA Ops:
  7.2 0.0 copy-start
  7.2 0.0 all-reduce.5.cloned.1.call-start
  7.2 2.6 collective-permute-start
  9.8 5.2 collective-permute-done
  15.0 0.0 collective-permute-start.1
  15.0 4.4 collective-permute-done.1
  19.4 0.0 collective-permute-start.2
  19.4 4.4 collective-permute-done.2
  23.8 0.0 collective-permute-start.3
  23.8 4.4 collective-permute-done.3
  28.1 0.0 collective-permute-start.4
  28.1 0.7 fusion.23
  28.8 3.7 collective-permute-done.4
  32.5 0.0 collective-permute-start.5
  33.2 3.7 collective-permute-done.5
  36.9 0.0 collective-permute-start.6
  36.9 1.3 dynamic-slice
  38.2 3.0 collective-permute-done.6
  41.3 0.7 constant_dynamic-update-slice_fusion
  42.1 0.1 copy_bitcast_fusion
  42.1 2.0 gather_fusion
  44.1 0.0 copy-done
  44.1 5.3 fusion.4
  49.5 0.0 copy-start.3
  49.5 5.1 copy.18
  54.5 0.0 copy-done.3
  54.5 5.1 fusion.17
  59.6 248.9 %all-reduce.6 = bf16[64,8192]{1,0:T(8,128)(2,1)} all-reduce(f32[64,8192]{1,0:T(8,128)} %fusion.17), channel_id=2, replica_groups=mesh['col'=64,'row'=8] {'col'}, use_global_device_ids=true, to_apply=%region_0.2.clone | all-reduce | flops 524288 | bytes 3145728
  308.5 1.6 fusion.13
  310.1 0.1 convert_element_type.27
  310.2 0.0 copy-start.1
  310.2 53.6 %collective-permute-start.7 = (bf16[128,64]{1,0:T(8,128)(2,1)S(1)}, bf16[128,64]{1,0:T(8,128)(2,1)S(1)}, u32[]{:S(2)}, u32[]{:S(2)}) collective-permute-start(bf16[128,64]{1,0:T(8,128)(2,1)S(1)} %convert_element_type.27), channel_id=1, source_target_pairs={{0,1},{1,2},{2,3},{3,4},{4,5},{5,6},{6,7},{7,0},{8,9},{9,10},{10,1... | collective-permute-start | bytes 49160 | tf_op jit(solution)/shard_map/ppermute | solution.py:28
  363.8 4.7 collective-permute-done.7
  368.6 0.0 collective-permute-start.8
  368.6 4.5 collective-permute-done.8
  373.1 0.0 collective-permute-start.9
  373.1 4.5 collective-permute-done.9
  377.7 0.0 collective-permute-start.10
  377.7 4.5 collective-permute-done.10
  382.2 0.0 collective-permute-start.11
  382.2 4.5 collective-permute-done.11
  386.8 0.0 collective-permute-start.12
  386.8 4.5 collective-permute-done.12
  391.3 0.0 collective-permute-start.13
  391.3 4.5 collective-permute-done.13
  396.0 0.9 fusion.10
  396.9 0.0 copy-done.1
  396.9 0.1 copy.20
  397.1 2.0 gather_fusion.1
  399.0 5.3 fusion.7
  404.4 5.1 copy.21
  409.4 0.0 copy-start.2
  409.4 5.1 fusion.15
  414.5 0.0 all-reduce.5.cloned.1.call-update
  414.5 259.6 %all-reduce.5.cloned.1.call-done = f32[64,8192]{1,0:T(8,128)} async-done(((f32[64,8192]{1,0:T(8,128)}), f32[64,8192]{1,0:T(8,128)}) %all-reduce.5.cloned.1.call-update) | async-done | bytes 2097168
  674.1 1.7 convert_reduce_fusion
  675.8 0.1 convert_element_type.29
  675.9 0.7 copy.22
  676.6 1.7 dynamic-slice_reduce_fusion
  678.3 0.1 squeeze_reshape.3
  678.4 0.0 copy-done.2
  678.4 0.2 fusion.24
  678.6 109.7 %psum.7 = f32[64,64]{1,0:T(8,128)S(1)} all-reduce(f32[64,64]{1,0:T(8,128)S(1)} %fusion.24), channel_id=1, replica_groups=mesh['col'=64,'row'=8] {'col','row'}, use_global_device_ids=true, to_apply=%region_2.4 | all-reduce | flops 4096 | bytes 32768 | tf_op jit(solution)/shard_map/psum | solution.py:44
  788.3 0.6 broadcast_multiply_fusion
  (17 shorter events, 0.2 us)
Async XLA Ops:
  7.2 37.0 %copy-start = (bf16[1,1,96,128,128]{4,3,2,1,0:T(8,128)(2,1)S(1)}, bf16[1,1,96,128,128]{4,3,2,1,0:T(8,128)(2,1)}, u32[]{:S(2)}) copy-start(bf16[1,1,96,128,128]{4,3,2,1,0:T(8,128)(2,1)} %param.8) | copy-start | bytes 9437188
  7.2 667.0 %all-reduce.5.cloned.1.call-start = ((), (), s32[]{:S(2)}) async-start(), calls=%async_computation | async-start | bytes 4194304
  7.2 7.8 collective-permute-start
  15.0 4.4 collective-permute-start.1
  19.4 4.4 collective-permute-start.2
  23.8 4.4 collective-permute-start.3
  28.1 4.4 collective-permute-start.4
  32.5 4.4 collective-permute-start.5
  36.9 4.4 collective-permute-start.6
  49.5 5.1 copy-start.3
  310.2 86.7 %copy-start.1 = (bf16[128,64]{1,0:T(8,128)(2,1)}, bf16[128,64]{1,0:T(8,128)(2,1)S(1)}, u32[]{:S(2)}) copy-start(bf16[128,64]{1,0:T(8,128)(2,1)S(1)} %convert_element_type.27) | copy-start | bytes 49156
  310.2 58.3 %collective-permute-start.7 = (bf16[128,64]{1,0:T(8,128)(2,1)S(1)}, bf16[128,64]{1,0:T(8,128)(2,1)S(1)}, u32[]{:S(2)}, u32[]{:S(2)}) collective-permute-start(bf16[128,64]{1,0:T(8,128)(2,1)S(1)} %convert_element_type.27), channel_id=1, source_target_pairs={{0,1},{1,2},{2,3},{3,4},{4,5},{5,6},{6,7},{7,0},{8,9},{9,10},{10,1... | collective-permute-start | bytes 49160 | tf_op jit(solution)/shard_map/ppermute | solution.py:28
  368.6 4.5 collective-permute-start.8
  373.1 4.6 collective-permute-start.9
  377.7 4.6 collective-permute-start.10
  382.2 4.5 collective-permute-start.11
  386.8 4.6 collective-permute-start.12
  391.3 4.5 collective-permute-start.13
  409.4 269.0 %copy-start.2 = (bf16[128,64]{1,0:T(8,128)(2,1)S(1)}, bf16[128,64]{1,0:T(8,128)(2,1)}, u32[]{:S(2)}) copy-start(bf16[128,64]{1,0:T(8,128)(2,1)} %copy-done.1) | copy-start | bytes 49156
Sparse Core Ops, SparseCore 0:
  414.6 259.4 all-reduce.4

commit v3 on v0

--- a/solution.py
+++ b/solution.py
@@ -30,7 +30,8 @@
     first = apply_local(x_block).astype(jnp.bfloat16)
     second = apply_local(first)
     gram_term = jnp.dot(first[0].astype(jnp.float32).T, second[0], precision=lax.Precision.HIGHEST)
-    gram = lax.psum(gram_term, ("col", "row")) / (n_col * n_row * 128)
+    search_gates = lambda view: lax.psum(lax.psum(view, "row"), "col")
+    gram = search_gates(gram_term) / (n_col * n_row * 128)
     return (second.astype(jnp.bfloat16), gram)
 
 

time: 761 us -> 957 us (1.26)
  the two profiles are of different devices: /device:TPU:1 before, /device:TPU:2 now
where the time goes in v3:
time: 957 us
  blocking collectives  630 us (66%)
  waiting for transfers between devices  267 us (28%)
  local copies, waits for them, and re-layouts  21.7 us (2%)
  matrix products  21.1 us (2%)
  between operations  14.9 us (2%)
    unnamed x1, blocking collectives  305 us
    psum x2, blocking collectives, local(): search_gates = lambda view: lax.psum(lax.psum(view, 'row'), 'col')  297 us
    unnamed x2, waiting for transfers between devices  267 us
    all_gather x2, blocking collectives, apply_local(): slab_vecs = lax.all_gather(segment[0], 'row', axis=0, tiled=True)  27.4 us
  transfers between devices with their start and end apart: 1, of which 1 were waited for; matrix products, arithmetic and copies ran while one was open for 0% of the time, Pallas kernels for 0%

profile of v3, /device:TPU:2, one launch (start us, length us, event | category | flops | bytes accessed | tf_op | source)
XLA Modules:
  0.0 956.6 jit_solution(5934625358005373638)
XLA Ops:
  7.2 0.0 copy-start
  7.2 0.0 all-reduce.5.cloned.1.call-start
  8.0 0.7 fusion.20
  8.8 15.1 %all-gather = bf16[1,1024,64]{1,2,0:T(8,128)(2,1)S(1)} all-gather(bf16[1,128,64]{1,2,0:T(8,128)(2,1)} %param.5), channel_id=2, replica_groups=mesh['col'=64,'row'=8] {'row'}, dimensions={1}, use_global_device_ids=true | all-gather | bytes 147456 | tf_op jit(solution)/shard_map/all_gather | solution.py:22
  24.0 2.0 gather_fusion
  25.9 0.0 copy-done
  25.9 5.3 fusion.4
  31.3 0.0 copy-start.3
  31.3 5.1 copy.18
  36.3 0.0 copy-done.3
  36.3 5.1 fusion.14
  41.4 305.4 %all-reduce.6 = bf16[64,8192]{1,0:T(8,128)(2,1)} all-reduce(f32[64,8192]{1,0:T(8,128)} %fusion.14), channel_id=3, replica_groups=mesh['col'=64,'row'=8] {'col'}, use_global_device_ids=true, to_apply=%region_0.0.clone | all-reduce | flops 524288 | bytes 3145728
  346.9 1.3 dynamic-slice
  348.2 1.7 fusion.10
  349.9 0.1 convert_element_type.27
  350.0 0.0 copy-start.1
  350.0 12.2 %all_gather.7 = bf16[1024,64]{1,0:T(8,128)(2,1)S(1)} all-gather(bf16[128,64]{1,0:T(8,128)(2,1)S(1)} %convert_element_type.27), channel_id=1, replica_groups=mesh['col'=64,'row'=8] {'row'}, dimensions={0}, use_global_device_ids=true | all-gather | bytes 147456 | tf_op jit(solution)/shard_map/all_gather | solution.py:22
  362.2 0.0 copy-done.1
  362.2 0.1 copy.20
  362.4 2.0 gather_fusion.1
  364.3 5.3 fusion.7
  369.7 5.1 copy.21
  374.7 0.0 copy-start.2
  374.7 5.1 fusion.12
  379.8 0.0 all-reduce.5.cloned.1.call-update
  379.8 267.4 %all-reduce.5.cloned.1.call-done = f32[64,8192]{1,0:T(8,128)} async-done(((f32[64,8192]{1,0:T(8,128)}), f32[64,8192]{1,0:T(8,128)}) %all-reduce.5.cloned.1.call-update) | async-done | bytes 2097168
  647.3 1.7 convert_reduce_fusion
  649.0 0.1 convert_element_type.29
  649.1 0.7 copy.22
  649.8 1.7 dynamic-slice_reduce_fusion
  651.5 0.1 squeeze_reshape.3
  651.6 0.0 copy-done.2
  651.6 0.2 fusion.21
  651.8 20.7 %psum.14 = f32[64,64]{1,0:T(8,128)S(1)} all-reduce(f32[64,64]{1,0:T(8,128)S(1)} %fusion.21), channel_id=1, replica_groups=mesh['col'=64,'row'=8] {'row'}, use_global_device_ids=true, to_apply=%region_2.0 | all-reduce | flops 4096 | bytes 32768 | tf_op jit(solution)/shard_map/psum | solution.py:33
  672.5 276.7 %psum.15 = f32[64,64]{1,0:T(8,128)S(1)} all-reduce(f32[64,64]{1,0:T(8,128)S(1)} %psum.14), channel_id=1, replica_groups=mesh['col'=64,'row'=8] {'col'}, use_global_device_ids=true, to_apply=%region_3.0 | all-reduce | flops 4096 | bytes 32768 | tf_op jit(solution)/shard_map/psum | solution.py:33
  949.2 0.6 broadcast_multiply_fusion
  (4 shorter events, 0.1 us)
Async XLA Ops:
  7.2 18.8 %copy-start = (bf16[1,1,96,128,128]{4,3,2,1,0:T(8,128)(2,1)S(1)}, bf16[1,1,96,128,128]{4,3,2,1,0:T(8,128)(2,1)}, u32[]{:S(2)}) copy-start(bf16[1,1,96,128,128]{4,3,2,1,0:T(8,128)(2,1)} %param.6) | copy-start | bytes 9437188
  7.2 640.1 %all-reduce.5.cloned.1.call-start = ((), (), s32[]{:S(2)}) async-start(), calls=%async_computation | async-start | bytes 4194304
  31.3 5.1 copy-start.3
  350.0 12.2 %copy-start.1 = (bf16[128,64]{1,0:T(8,128)(2,1)}, bf16[128,64]{1,0:T(8,128)(2,1)S(1)}, u32[]{:S(2)}) copy-start(bf16[128,64]{1,0:T(8,128)(2,1)S(1)} %convert_element_type.27) | copy-start | bytes 49156
  374.7 276.9 %copy-start.2 = (bf16[128,64]{1,0:T(8,128)(2,1)S(1)}, bf16[128,64]{1,0:T(8,128)(2,1)}, u32[]{:S(2)}) copy-start(bf16[128,64]{1,0:T(8,128)(2,1)} %copy-done.1) | copy-start | bytes 49156
Sparse Core Ops, SparseCore 0:
  380.0 267.2 all-reduce.4
